TPU v7x, 512 devices: a whole 4x4x16 slice. The times are simulated.
512 devices in a mesh: grp: 16 (over y, x), tok: 32 (over z, core).
Axes of the slice: x: 4, y: 4, z: 16, core: 2. Of those that a mesh axis runs over, the one named last changes fastest.
Arguments:
- hidden_in: bfloat16 [16, 4096, 1024], P('grp', 'tok'), may hold values from -6 to 6
- lengths: int32 [16, 3], P('grp'), may hold values from 1 to 3072, 4096 in all within a row
- prefix_cache: bfloat16 [16, 512, 512], P('grp', 'tok'), may hold values from -2600 to 2600
- routes: int32 [16, 4096, 8], P('grp', 'tok'), may hold values from 0 to 31, all different within a row; in each aligned block of 128 rows (0 to 127, 128 to 255, ..., all dimensions but the last counted through in order) at most 40 rows name the same one
- gates: float32 [16, 4096, 8], P('grp', 'tok'), may hold values from 0.05 to 0.4
- attn_gain: float32 [1024], replicated, may hold values from 0.1 to 1.9
- w_qkv: bfloat16 [1024, 1024], P('grp', 'tok'), may hold values from -0.75 to 0.75
- w_out: bfloat16 [512, 1024], P('grp', 'tok'), may hold values from -0.25 to 0.25
- moe_gain: float32 [1024], replicated, may hold values from 0.1 to 1.9
- expert_gate_up: bfloat16 [32, 1024, 1024], P('tok', 'grp'), may hold values from -0.1875 to 0.1875
- expert_down: bfloat16 [32, 512, 1024], P('tok', 'grp'), may hold values from -0.25 to 0.25
Outputs:
- hidden_out: bfloat16 [16, 4096, 1024], P('grp', 'tok')
- suffix_cache: bfloat16 [16, 4096, 512], P('grp', 'tok')
Inputs may be any that keep to these rules, and one draw needn't show every extreme that they name: Each group's 3 lengths sum to 4096; no request is longer than 3072 tokens, and some request of every draw has exactly 3072. `routes`: each token names 8 different experts. Among the 128 tokens of one device no expert is named more than 40 times, a bound that some block reaches.
All inputs are finite; a program needn't handle non-finite values.
Results may differ from a plain program's by a relative error of at most 0.02.
Values may be sent and summed in bfloat16 or wider, within the bound.
A program may use at most 128 MiB of HBM per device.

v0:
```python
import jax
import jax.numpy as jnp
from jax import lax
from jax.sharding import PartitionSpec as P

HEADS = 8
KV_HEADS = 4
HEAD_DIM = 64
FF = 512
EXPERTS = 32
TOP = 8
CAP = 40
epsilon = 1e-05
score_scale = 0.015625
rope_base = 10000.0
big_negative = -1e30


def rms_scale(values, gain):
    values = values.astype(jnp.float32)
    mean_square = jnp.mean(values * values, axis=-1, keepdims=True)
    return values * lax.rsqrt(mean_square + epsilon) * gain


def request_layout(group_lengths, token_index):
    ends = jnp.cumsum(group_lengths)
    starts = ends - group_lengths
    segment = jnp.sum((token_index[:, None] >= ends[None, :]).astype(jnp.int32), axis=1)
    match = segment[:, None] == jnp.arange(group_lengths.shape[0], dtype=jnp.int32)[None, :]
    offset = token_index - jnp.sum(jnp.where(match, starts[None, :], 0), axis=1)
    return (segment, offset)


def rotate(values, position):
    half_width = values.shape[-1] // 2
    frequency = rope_base ** (-jnp.arange(half_width, dtype=jnp.float32) * 2.0 / values.shape[-1])
    angle = position.astype(jnp.float32)[:, None] * frequency[None, :]
    cosine = jnp.cos(angle)[:, None, :]
    sine = jnp.sin(angle)[:, None, :]
    first = values[..., :half_width]
    second = values[..., half_width:]
    return jnp.concatenate(
        [first * cosine - second * sine, second * cosine + first * sine], axis=-1
    )


def attend(carry, grouped, keys_values, allowed):
    best, total, mixed = carry
    key_count = keys_values.shape[0]
    key_width = KV_HEADS * HEAD_DIM
    key_heads = keys_values[:, :key_width].reshape(key_count, KV_HEADS, HEAD_DIM).transpose(1, 0, 2)
    value_heads = (
        keys_values[:, key_width:].reshape(key_count, KV_HEADS, HEAD_DIM).transpose(1, 0, 2)
    )
    scores = (
        jnp.einsum("kqd,knd->kqn", grouped, key_heads, preferred_element_type=jnp.float32)
        * score_scale
    )
    if allowed is not None:
        row_count = grouped.shape[1]
        share = row_count // allowed.shape[0]
        mask = jnp.broadcast_to(allowed[:, None, :], (allowed.shape[0], share, key_count)).reshape(
            row_count, key_count
        )
        scores = jnp.where(mask[None], scores, big_negative)
    new_best = jnp.maximum(best, jnp.max(scores, axis=-1))
    factor = jnp.exp(best - new_best)
    probs = jnp.exp(scores - new_best[..., None])
    total = total * factor + jnp.sum(probs, axis=-1)
    mixed = mixed * factor[..., None] + jnp.einsum(
        "kqn,knd->kqd", probs.astype(jnp.bfloat16), value_heads, preferred_element_type=jnp.float32
    )
    return (new_best, total, mixed)


def local(
    hidden_in,
    lengths,
    prefix_cache,
    routes,
    gates,
    attn_gain,
    w_qkv,
    w_out,
    moe_gain,
    expert_gate_up,
    expert_down,
):
    tokens_here = hidden_in[0]
    tok_count = tokens_here.shape[0]
    axis_count = lax.axis_size("tok")
    device_place = lax.axis_index("tok")
    group_lengths = lengths[0]
    token_index = device_place * tok_count + jnp.arange(tok_count, dtype=jnp.int32)
    segment, offset = request_layout(group_lengths, token_index)
    position = prefix_cache.shape[1] * axis_count + offset
    query_width = HEADS * HEAD_DIM
    key_width = KV_HEADS * HEAD_DIM
    group_share = HEADS // KV_HEADS
    normed = rms_scale(tokens_here, attn_gain).astype(jnp.bfloat16)
    columns = lax.all_gather(w_qkv, "tok", axis=1, tiled=True)
    sliced = normed
    projected = jnp.dot(
        sliced,
        lax.all_gather(columns, "grp", axis=0, tiled=True),
        preferred_element_type=jnp.float32,
    )
    query = rotate(projected[:, :query_width].reshape(tok_count, HEADS, HEAD_DIM), position).astype(
        jnp.bfloat16
    )
    keys_new = rotate(
        projected[:, query_width : query_width + key_width].reshape(tok_count, KV_HEADS, HEAD_DIM),
        position,
    ).astype(jnp.bfloat16)
    values_new = projected[:, query_width + key_width :].astype(jnp.bfloat16)
    suffix_cache = jnp.concatenate([keys_new.reshape(tok_count, key_width), values_new], axis=1)
    row_count = tok_count * group_share
    grouped = (
        query.reshape(tok_count, KV_HEADS, group_share, HEAD_DIM)
        .transpose(1, 0, 2, 3)
        .reshape(KV_HEADS, row_count, HEAD_DIM)
    )
    start_carry = (
        jnp.full((KV_HEADS, row_count), big_negative, jnp.float32),
        jnp.zeros((KV_HEADS, row_count), jnp.float32),
        jnp.zeros((KV_HEADS, row_count, HEAD_DIM), jnp.float32),
    )
    carry = attend(
        start_carry, grouped, lax.all_gather(prefix_cache[0], "tok", axis=0, tiled=True), None
    )
    piece = lax.all_gather(suffix_cache, "tok", axis=0, tiled=True)
    key_index = jnp.arange(piece.shape[0], dtype=jnp.int32)
    key_segment, key_offset = request_layout(group_lengths, key_index)
    earlier = key_index[None, :] <= token_index[:, None]
    same_request = key_segment[None, :] == segment[:, None]
    carry = attend(carry, grouped, piece, earlier & same_request & (key_index[None, :] >= 0))
    best, total, mixed = carry
    attended = (mixed / total[..., None]).reshape(KV_HEADS, tok_count, group_share, HEAD_DIM)
    attended = attended.transpose(1, 0, 2, 3).reshape(tok_count, query_width).astype(jnp.bfloat16)
    out_columns = lax.all_gather(w_out, "tok", axis=1, tiled=True)
    sliced = attended
    projected_out = jnp.dot(
        sliced,
        lax.all_gather(out_columns, "grp", axis=0, tiled=True),
        preferred_element_type=jnp.float32,
    )
    after_attention = tokens_here.astype(jnp.float32) + projected_out
    moe_in = rms_scale(after_attention, moe_gain).astype(jnp.bfloat16)
    model_width = moe_in.shape[1]
    flat_routes = routes[0].reshape(-1)
    onehot = (flat_routes[:, None] == jnp.arange(EXPERTS, dtype=jnp.int32)[None, :]).astype(
        jnp.int32
    )
    slot_rank = jnp.sum(jnp.cumsum(onehot, axis=0) * onehot, axis=1) - 1
    slot_index = flat_routes * CAP + slot_rank
    source_token = jnp.arange(flat_routes.shape[0], dtype=jnp.int32) // TOP
    outgoing = (
        jnp.zeros((EXPERTS * CAP, model_width), jnp.bfloat16)
        .at[slot_index]
        .set(moe_in[source_token])
    )
    arrived = lax.all_to_all(
        outgoing.reshape(EXPERTS, CAP, model_width), "tok", split_axis=0, concat_axis=1, tiled=True
    )
    sliced = arrived
    hidden_pair = jnp.einsum(
        "erd,edf->erf",
        sliced,
        lax.all_gather(expert_gate_up, "grp", axis=1, tiled=True),
        preferred_element_type=jnp.float32,
    )
    activated = (jax.nn.silu(hidden_pair[..., :FF]) * hidden_pair[..., FF:]).astype(jnp.bfloat16)
    sliced = activated
    expert_result = jnp.einsum(
        "erf,efd->erd",
        sliced,
        lax.all_gather(expert_down, "grp", axis=1, tiled=True),
        preferred_element_type=jnp.float32,
    ).astype(jnp.bfloat16)
    returned = lax.all_to_all(
        expert_result, "tok", split_axis=1, concat_axis=0, tiled=True
    ).reshape(EXPERTS * CAP, -1)
    weighted = returned[slot_index].astype(jnp.float32) * gates[0].reshape(-1)[:, None]
    moe_out = jnp.sum(weighted.reshape(tok_count, TOP, -1), axis=1)
    hidden_out = (after_attention + moe_out).astype(jnp.bfloat16)
    return (hidden_out[None], suffix_cache[None])


def solution(mesh):
    return jax.shard_map(
        local,
        mesh=mesh,
        in_specs=(
            P("grp", "tok", None),
            P("grp", None),
            P("grp", "tok", None),
            P("grp", "tok", None),
            P("grp", "tok", None),
            P(),
            P("grp", "tok"),
            P("grp", "tok"),
            P(),
            P("tok", "grp", None),
            P("tok", "grp", None),
        ),
        out_specs=(P("grp", "tok", None), P("grp", "tok", None)),
        check_vma=False,
    )
```

profile of v0, /device:TPU:32, one launch (start us, length us, event | category | flops | bytes accessed | tf_op | source)
XLA Modules:
  0.0 593.4 jit_solution(6562197188762396571)
XLA Ops:
  7.2 35.0 %all_gather.24 = bf16[64,1024]{0,1:T(8,128)(2,1)S(1)} all-gather(bf16[64,32]{0,1:T(8,128)(2,1)} %param.17), channel_id=1, replica_groups=mesh['grp'=16,'tok'=32] {'tok'}, dimensions={1}, use_global_device_ids=true | all-gather | bytes 135168 | tf_op jit(solution)/shard_map/all_gather | solution.py:101
  46.1 55.2 %all-gather.7.cloned.1.call-done = bf16[1024,1024]{1,0:T(8,128)(2,1)} async-done(((bf16[64,1024]{1,0:T(8,128)(2,1)}), bf16[1024,1024]{1,0:T(8,128)(2,1)}) %all-gather.7.cloned.1.call-update) | async-done | bytes 2097168 | tf_op jit(solution)/shard_map/all_gather | solution.py:105
  101.3 2.2 fusion.30
  105.4 30.6 %all_gather.28 = bf16[32,1024]{0,1:T(8,128)(2,1)S(1)} all-gather(bf16[32,32]{0,1:T(8,128)(2,1)S(1)} %copy.120), channel_id=1, replica_groups=mesh['grp'=16,'tok'=32] {'tok'}, dimensions={1}, use_global_device_ids=true | all-gather | bytes 67584 | tf_op jit(solution)/shard_map/all_gather | solution.py:140
  137.7 2.4 broadcast_in_dim.41
  140.2 2.6 broadcast_in_dim.42
  142.7 31.0 %all-gather = bf16[1,512,512]{2,1,0:T(8,128)(2,1)S(1)} all-gather(bf16[1,16,512]{2,1,0:T(8,128)(2,1)S(1)} %copy-done.5), channel_id=2, replica_groups=mesh['grp'=16,'tok'=32] {'tok'}, dimensions={1}, use_global_device_ids=true | all-gather | bytes 540672 | tf_op jit(solution)/shard_map/all_gather | solution.py:129
  175.0 9.2 %reduce-window.11 = s32[32,8,128]{2,1,0:T(8,128)S(1)} reduce-window(s32[32,8,128]{2,1,0:T(8,128)S(1)} %fusion.37, s32[]{:T(128)} %constant.34.clone.1), window={size=1x1x128 pad=0_0x0_0x127_0}, to_apply=%region_9.10 | reduce-window | flops 4161536 | bytes 262148 | tf_op jit(solution)/shard_map/reduce-window.1
  186.0 1.8 multiply_reduce_fusion
  187.8 3.8 fusion.45
  191.6 2.9 copy.117
  194.6 2.9 copy.115
  197.5 3.5 fusion
  201.0 4.4 fusion.1
  205.4 1.9 copy-done
  207.9 11.2 %fusion.3 = f32[4,256,64]{1,2,0:T(8,128)} fusion(bf16[4,4096,64]{1,2,0:T(8,128)(2,1)} %bitcast.105, f32[4,256,4096]{2,1,0:T(8,128)} %copy-done, f32[4,256]{1,0:T(4,128)S(1)} %get-tuple-element.15, pred[256,4096]{1,0:T(8,128)(4,1)S(1)} %broadcast_in_dim.42), kind=kOutput, calls=%fused_computation.8 | convolution fusion | flops 553648128 | bytes 20189184 | tf_op jit(solution)/shard_map/kqn,knd->kqd/dot_general | solution.py:70
  221.0 16.5 %all-gather.11.cloned.1.call-done = bf16[512,1024]{1,0:T(8,128)(2,1)} async-done(((bf16[32,1024]{1,0:T(8,128)(2,1)}), bf16[512,1024]{1,0:T(8,128)(2,1)}) %all-gather.11.cloned.1.call-update) | async-done | bytes 1048592 | tf_op jit(solution)/shard_map/all_gather | solution.py:144
  239.3 14.7 %scatter_custom_fusion = bf16[1280,1024]{1,0:T(8,128)(2,1)} fusion(s32[1024]{0:T(1024)S(1)} %bitcast.118, bf16[128,1024]{1,0:T(8,128)(2,1)S(1)} %multiply_convert_fusion, s32[1024]{0:T(1024)S(1)} %broadcast_clamp_fusion.1, bf16[]{:T(256)} %constant.67.clone.1), kind=kCustom, calls=%fused_computation.19 | custom fusion | bytes 2621442 | tf_op jit(solution)/shard_map/scatter | solution.py:160
  254.1 12.8 %all-to-all-start = ((bf16[32,40,1024]{2,1,0:T(8,128)(2,1)}), bf16[32,40,1024]{2,1,0:T(8,128)(2,1)S(1)}, u32[]{:S(2)}, u32[]{:S(2)}) async-start(bf16[32,40,1024]{2,1,0:T(8,128)(2,1)} %bitcast.31), calls=%async_computation | async-start | bytes 5242880 | tf_op jit(solution)/shard_map/all_to_all | solution.py:162
  268.0 61.4 %all-gather.13.cloned.1.call-done = bf16[1,1024,1024]{2,1,0:T(8,128)(2,1)} async-done(((bf16[1,64,1024]{2,1,0:T(8,128)(2,1)}), bf16[1,1024,1024]{2,1,0:T(8,128)(2,1)}) %all-gather.13.cloned.1.call-update) | async-done | bytes 2097168 | tf_op jit(solution)/shard_map/all_gather | solution.py:169
  329.4 60.2 %all-to-all-done = bf16[32,40,1024]{2,1,0:T(8,128)(2,1)S(1)} async-done(((bf16[32,40,1024]{2,1,0:T(8,128)(2,1)}), bf16[32,40,1024]{2,1,0:T(8,128)(2,1)S(1)}, u32[]{:S(2)}, u32[]{:S(2)}) %all-to-all-start) | async-done | bytes 2621472 | tf_op jit(solution)/shard_map/all_to_all | solution.py:162
  389.6 6.2 %convolution_bitcast_fusion = f32[1,1280,1024]{2,1,0:T(8,128)} fusion(bf16[1280,1024]{1,0:T(8,128)(2,1)S(1)} %bitcast.104, bf16[1,1024,1024]{2,1,0:T(8,128)(2,1)} %all-gather.13.cloned.1.call-done), kind=kOutput, calls=%fused_computation.10 | convolution fusion | flops 2684354560 | bytes 9961472 | tf_op jit(solution)/shard_map/erd,edf->erf/dot_general | solution.py:166
  395.8 4.4 fusion.7
  400.2 18.2 %copy.137 = bf16[1,1280,1024]{2,0,1:T(2,128)(2,1)} copy(bf16[1,1280,1024]{2,1,0:T(8,128)(2,1)S(1)} %fusion.7) | data formatting | bytes 5242880 | tf_op jit(solution)/shard_map/convert_element_type | solution.py:179
  418.9 15.6 %reduce = bf16[1280,1024]{1,0:T(8,128)(2,1)S(1)} reduce(bf16[1280,1,1024]{2,1,0:T(2,128)(2,1)} %bitcast.99, bf16[]{:T(256)} %broadcast.297), dimensions={1}, to_apply=%bitcast.97.reduce_sub_computation | reduce | bytes 5242882
  434.4 3.0 reshape.386
  437.4 6.9 %all-to-all-start.1 = ((bf16[32,2,20480]{2,1,0:T(2,128)(2,1)}), bf16[32,2,20480]{2,1,0:T(2,128)(2,1)S(1)}, u32[]{:S(2)}, u32[]{:S(2)}) async-start(bf16[32,2,20480]{2,1,0:T(2,128)(2,1)} %reshape.386), calls=%async_computation.1 | async-start | bytes 5242880 | tf_op jit(solution)/shard_map/all_to_all | solution.py:180
  444.5 122.6 %all-to-all-done.1 = bf16[32,2,20480]{2,1,0:T(2,128)(2,1)S(1)} async-done(((bf16[32,2,20480]{2,1,0:T(2,128)(2,1)}), bf16[32,2,20480]{2,1,0:T(2,128)(2,1)S(1)}, u32[]{:S(2)}, u32[]{:S(2)}) %all-to-all-start.1) | async-done | bytes 2621472 | tf_op jit(solution)/shard_map/all_to_all | solution.py:180
  567.1 7.2 %reshape.387 = bf16[1280,1,1024]{2,1,0:T(2,128)(2,1)} reshape(bf16[32,2,20480]{2,1,0:T(2,128)(2,1)S(1)} %all-to-all-done.1) | data formatting | bytes 5242880
  574.3 3.5 copy.136
  577.8 5.4 gather_fusion
  583.2 2.9 fusion.6
  (94 shorter events, 17.1 us)
Async XLA Ops:
  7.2 94.1 %all-gather.7.cloned.1.call-start = ((), (), s32[]{:S(2)}) async-start(), calls=%async_computation.2 | async-start | bytes 2228224 | tf_op jit(solution)/shard_map/all_gather | solution.py:105
  42.3 63.1 %copy-start.7 = (bf16[32,32]{1,0:T(8,128)(2,1)S(1)}, bf16[32,32]{1,0:T(8,128)(2,1)}, u32[]{:S(2)}) copy-start(bf16[32,32]{1,0:T(8,128)(2,1)} %param.18) | copy-start | bytes 6148
  43.1 144.7 %all-gather.9.cloned.1.call-start = ((), (), s32[]{:S(2)}) async-start(), calls=%async_computation.3 | async-start | bytes 4325376 | tf_op jit(solution)/shard_map/all_gather | solution.py:131
  46.1 90.9 %copy-start.6 = (s32[1,128,8]{1,2,0:T(8,128)S(1)}, s32[1,128,8]{1,2,0:T(8,128)}, u32[]{:S(2)}) copy-start(s32[1,128,8]{1,2,0:T(8,128)} %param.14) | copy-start | bytes 12292
  103.5 0.8 copy-start.3
  105.3 132.3 %all-gather.11.cloned.1.call-start = ((), (), s32[]{:S(2)}) async-start(), calls=%async_computation.4 | async-start | bytes 1114112 | tf_op jit(solution)/shard_map/all_gather | solution.py:144
  137.7 5.0 copy-start.5
  142.7 42.0 %slice-start = ((f32[128,1024]{1,0:T(8,128)}), f32[128,512]{1,0:T(8,128)S(1)}, s32[]{:S(2)}) async-start(f32[128,1024]{1,0:T(8,128)} %copy-done.3), calls=%async_computation.7 | async-start | bytes 524288 | tf_op jit(solution)/shard_map/slice | solution.py:108
  201.0 6.3 %copy-start = (f32[4,256,4096]{2,1,0:T(8,128)}, f32[4,256,4096]{2,1,0:T(8,128)S(1)}, u32[]{:S(2)}) copy-start(f32[4,256,4096]{2,1,0:T(8,128)S(1)} %get-tuple-element.22) | copy-start | bytes 50331652
  201.0 6.3 %copy-start.1 = (f32[4,256,512]{2,1,0:T(8,128)S(1)}, f32[4,256,512]{2,1,0:T(8,128)}, u32[]{:S(2)}) copy-start(f32[4,256,512]{2,1,0:T(8,128)} %get-tuple-element.20) | copy-start | bytes 6291460
  207.9 11.2 %copy-start.4 = (bf16[512,256]{0,1:T(8,128)(2,1)S(1)}, bf16[512,256]{0,1:T(8,128)(2,1)}, u32[]{:S(2)}) copy-start(bf16[512,256]{0,1:T(8,128)(2,1)} %copy.112) | copy-start | bytes 786436
  219.1 18.4 %copy-start.2 = (bf16[1,128,1024]{2,1,0:T(8,128)(2,1)S(1)}, bf16[1,128,1024]{2,1,0:T(8,128)(2,1)}, u32[]{:S(2)}) copy-start(bf16[1,128,1024]{2,1,0:T(8,128)(2,1)} %param.11) | copy-start | bytes 786436
  219.1 20.1 %copy-start.8 = (f32[1024]{0:T(1024)S(1)}, f32[1024]{0:T(1024)}, u32[]{:S(2)}) copy-start(f32[1024]{0:T(1024)} %param.19) | copy-start | bytes 12292
  254.1 135.6 %all-to-all-start = ((bf16[32,40,1024]{2,1,0:T(8,128)(2,1)}), bf16[32,40,1024]{2,1,0:T(8,128)(2,1)S(1)}, u32[]{:S(2)}, u32[]{:S(2)}) async-start(bf16[32,40,1024]{2,1,0:T(8,128)(2,1)} %bitcast.31), calls=%async_computation | async-start | bytes 5242880 | tf_op jit(solution)/shard_map/all_to_all | solution.py:162
  266.9 62.5 %all-gather.13.cloned.1.call-start = ((), (), s32[]{:S(2)}) async-start(), calls=%async_computation.5 | async-start | bytes 2228224 | tf_op jit(solution)/shard_map/all_gather | solution.py:169
  267.5 128.3 %all-gather.15.cloned.1.call-start = ((), (), s32[]{:S(2)}) async-start(), calls=%async_computation.6 | async-start | bytes 1114112 | tf_op jit(solution)/shard_map/all_gather | solution.py:177
  437.4 6.9 %copy-start.9 = (f32[1,128,8]{1,2,0:T(8,128)S(1)}, f32[1,128,8]{1,2,0:T(8,128)}, u32[]{:S(2)}) copy-start(f32[1,128,8]{1,2,0:T(8,128)} %param.15) | copy-start | bytes 12292
  437.4 129.7 %all-to-all-start.1 = ((bf16[32,2,20480]{2,1,0:T(2,128)(2,1)}), bf16[32,2,20480]{2,1,0:T(2,128)(2,1)S(1)}, u32[]{:S(2)}, u32[]{:S(2)}) async-start(bf16[32,2,20480]{2,1,0:T(2,128)(2,1)} %reshape.386), calls=%async_computation.1 | async-start | bytes 5242880 | tf_op jit(solution)/shard_map/all_to_all | solution.py:180
Sparse Core Ops, SparseCore 0:
  43.2 58.0 all-gather.6
  105.4 73.6 all-gather.8
  182.1 55.3 all-gather.10
  270.4 58.9 all-gather.12
  332.3 57.4 all-gather.14
where the time goes:
time: 594 us; the launch traced here: 593 us
  waiting for transfers between devices  317 us (53%)
  blocking collectives  96.7 us (16%)
  local copies, waits for them, and re-layouts  74.3 us (13%)
  other arithmetic  38.8 us (7%)
  matrix products  32.4 us (5%)
  starting transfers between devices  19.9 us (3%)
  between operations  14.2 us (2%)
    all_to_all x1, waiting for transfers between devices, local(): lax.all_to_all(expert_result, 'tok', split_axis=1, concat_axis=0, tiled=T...  123 us
    all_gather x1, waiting for transfers between devices, local(): lax.all_gather(expert_gate_up, 'grp', axis=1, tiled=True)  61.4 us
    all_to_all x1, waiting for transfers between devices, local(): lax.all_to_all(outgoing.reshape(EXPERTS, CAP, model_width), 'tok', split_...  60.2 us
    all_gather x1, waiting for transfers between devices, local(): lax.all_gather(columns, 'grp', axis=0, tiled=True)  55.2 us
    all_gather x1, blocking collectives, local(): columns = lax.all_gather(w_qkv, 'tok', axis=1, tiled=True)  35 us
    all_gather x1, blocking collectives, local(): lax.all_gather(prefix_cache[0], 'tok', axis=0, tiled=True)  31 us
    all_gather x1, blocking collectives, local(): out_columns = lax.all_gather(w_out, 'tok', axis=1, tiled=True)  30.6 us
    convert_element_type x1, local copies, waits for them, and re-layouts, local(): expert_result = jnp.einsum('erf,efd->erd', sliced, lax.all_gather(expert_...  18.2 us
  transfers between devices with their start and end apart: 7, of which 5 were waited for; matrix products, arithmetic and copies ran while one was open for 10% of the time, Pallas kernels for 0%

commit v1 on v0

--- a/solution.py
+++ b/solution.py
@@ -14,6 +14,22 @@
 score_scale = 0.015625
 rope_base = 10000.0
 big_negative = -1e30
+
+
+def product_in_turn(x, axis, dim, contribution):
+    devices, index, span = (lax.axis_size(axis), lax.axis_index(axis), x.shape[dim])
+    right = [(i, (i + 1) % devices) for i in range(devices)]
+    behind = [(i, (i - 1) % devices) for i in range(devices)]
+    half = devices // 2
+    from_left = from_right = x
+    so_far = contribution(x, index * span)
+    for lap in range(1, half + 1):
+        from_left = lax.ppermute(from_left, axis, right)
+        if lap < devices - half:
+            from_right = lax.ppermute(from_right, axis, behind)
+            so_far = so_far + contribution(from_right, (index + lap) % devices * span)
+        so_far = so_far + contribution(from_left, (index - lap) % devices * span)
+    return so_far
 
 
 def rms_scale(values, gain):
@@ -163,11 +179,16 @@
         outgoing.reshape(EXPERTS, CAP, model_width), "tok", split_axis=0, concat_axis=1, tiled=True
     )
     sliced = arrived
-    hidden_pair = jnp.einsum(
-        "erd,edf->erf",
-        sliced,
-        lax.all_gather(expert_gate_up, "grp", axis=1, tiled=True),
-        preferred_element_type=jnp.float32,
+    hidden_pair = product_in_turn(
+        expert_gate_up,
+        "grp",
+        1,
+        lambda own_block, start: jnp.einsum(
+            "erd,edf->erf",
+            lax.dynamic_slice_in_dim(sliced, start, own_block.shape[1], axis=2),
+            own_block,
+            preferred_element_type=jnp.float32,
+        ),
     )
     activated = (jax.nn.silu(hidden_pair[..., :FF]) * hidden_pair[..., FF:]).astype(jnp.bfloat16)
     sliced = activated

time: 594 us -> 669 us (1.13)
  matrix products: 32.4 us -> 106 us
  waiting for transfers between devices: 317 us -> 244 us
  starting transfers between devices: 19.9 us -> 83.4 us
    dot_general x1 -> x16, matrix products: 6.17 us -> 80.3 us  [local(): jnp.einsum('erd,edf->erf', lax.dynamic_slice_in_dim(sliced, start, own_bl...]
    ppermute x0 -> x15, starting transfers between devices: none -> 66.3 us  [the longest x7 49.8 us: product_in_turn(): from_right = lax.ppermute(from_right, axis, behind)]
    all_gather x1 -> x0, waiting for transfers between devices: 61.4 us -> none  [local(): lax.all_gather(expert_gate_up, 'grp', axis=1, tiled=True)]
    all_to_all x1, waiting for transfers between devices: 60.2 us -> 48.4 us  [local(): lax.all_to_all(outgoing.reshape(EXPERTS, CAP, model_width), 'tok', split_...]
    ppermute x0 -> x15, waiting for transfers between devices: none -> 7.44 us  [the longest x8 7.43 us: product_in_turn(): from_left = lax.ppermute(from_left, axis, right)]
    unnamed x26 -> x56, local copies, waits for them, and re-layouts: 17.1 us -> 16.3 us
  transfers between devices with their start and end apart: 7 -> 21, of which waited for: 5 -> 11; matrix products, arithmetic and copies ran while one was open for 10% -> 21% of each run, Pallas kernels for 0% -> 0%
where the time goes in v1:
time: 669 us; the launch traced here: 664 us
  waiting for transfers between devices  244 us (36%)
  matrix products  106 us (16%)
  blocking collectives  96.6 us (14%)
  starting transfers between devices  83.4 us (12%)
  local copies, waits for them, and re-layouts  80.5 us (12%)
  other arithmetic  38.6 us (6%)
  between operations  15 us (2%)
    all_to_all x1, waiting for transfers between devices, local(): lax.all_to_all(expert_result, 'tok', split_axis=1, concat_axis=0, tiled=T...  122 us
    dot_general x16, matrix products, local(): jnp.einsum('erd,edf->erf', lax.dynamic_slice_in_dim(sliced, start, own_bl...  80.3 us
    all_gather x1, waiting for transfers between devices, local(): lax.all_gather(columns, 'grp', axis=0, tiled=True)  55.2 us
    ppermute x7, starting transfers between devices, product_in_turn(): from_right = lax.ppermute(from_right, axis, behind)  49.8 us
    all_to_all x1, waiting for transfers between devices, local(): lax.all_to_all(outgoing.reshape(EXPERTS, CAP, model_width), 'tok', split_...  48.4 us
    all_gather x1, blocking collectives, local(): columns = lax.all_gather(w_qkv, 'tok', axis=1, tiled=True)  35 us
    all_gather x1, blocking collectives, local(): lax.all_gather(prefix_cache[0], 'tok', axis=0, tiled=True)  31 us
    all_gather x1, blocking collectives, local(): out_columns = lax.all_gather(w_out, 'tok', axis=1, tiled=True)  30.6 us
  transfers between devices with their start and end apart: 21, of which 11 were waited for; matrix products, arithmetic and copies ran while one was open for 21% of the time, Pallas kernels for 0%

profile of v1, /device:TPU:32, one launch (start us, length us, event | category | flops | bytes accessed | tf_op | source)
XLA Modules:
  0.0 663.7 jit_solution(2571721629034677518)
XLA Ops:
  7.2 35.0 %all_gather.21 = bf16[64,1024]{0,1:T(8,128)(2,1)S(1)} all-gather(bf16[64,32]{0,1:T(8,128)(2,1)} %param.17), channel_id=1, replica_groups=mesh['grp'=16,'tok'=32] {'tok'}, dimensions={1}, use_global_device_ids=true | all-gather | bytes 135168 | tf_op jit(solution)/shard_map/all_gather | solution.py:117
  46.1 55.2 %all-gather.6.cloned.1.call-done = bf16[1024,1024]{1,0:T(8,128)(2,1)} async-done(((bf16[64,1024]{1,0:T(8,128)(2,1)}), bf16[1024,1024]{1,0:T(8,128)(2,1)}) %all-gather.6.cloned.1.call-update) | async-done | bytes 2097168 | tf_op jit(solution)/shard_map/all_gather | solution.py:121
  104.7 30.6 %all_gather.25 = bf16[32,1024]{0,1:T(8,128)(2,1)S(1)} all-gather(bf16[32,32]{0,1:T(8,128)(2,1)S(1)} %copy.120), channel_id=1, replica_groups=mesh['grp'=16,'tok'=32] {'tok'}, dimensions={1}, use_global_device_ids=true | all-gather | bytes 67584 | tf_op jit(solution)/shard_map/all_gather | solution.py:156
  140.8 5.4 broadcast_in_dim.42
  146.2 31.0 %all-gather = bf16[1,512,512]{2,1,0:T(8,128)(2,1)S(1)} all-gather(bf16[1,16,512]{2,1,0:T(8,128)(2,1)S(1)} %copy-done.20), channel_id=2, replica_groups=mesh['grp'=16,'tok'=32] {'tok'}, dimensions={1}, use_global_device_ids=true | all-gather | bytes 540672 | tf_op jit(solution)/shard_map/all_gather | solution.py:145
  177.6 9.0 %reduce-window.11 = s32[32,8,128]{2,1,0:T(8,128)S(1)} reduce-window(s32[32,8,128]{2,1,0:T(8,128)S(1)} %fusion.99, s32[]{:T(128)} %constant.147.clone.1), window={size=1x1x128 pad=0_0x0_0x127_0}, to_apply=%region_9.10 | reduce-window | flops 4161536 | bytes 262148 | tf_op jit(solution)/shard_map/reduce-window.1
  190.4 4.5 fusion.123
  194.8 4.1 copy.115
  199.0 4.1 copy.117
  203.1 4.7 fusion
  207.8 4.4 fusion.1
  214.7 8.6 %fusion.3 = f32[4,256,64]{1,2,0:T(8,128)S(1)} fusion(bf16[4,4096,64]{1,2,0:T(8,128)(2,1)} %bitcast.213, f32[4,256,4096]{2,1,0:T(8,128)} %copy-done, f32[4,256]{1,0:T(4,128)S(1)} %get-tuple-element.15, pred[256,4096]{1,0:T(8,128)(4,1)S(1)} %broadcast_in_dim.42), kind=kOutput, calls=%fused_computation.8 | convolution fusion | flops 553648128 | bytes 20189184 | tf_op jit(solution)/shard_map/kqn,knd->kqd/dot_general | solution.py:86
  225.9 10.4 %all-gather.10.cloned.1.call-done = bf16[512,1024]{1,0:T(8,128)(2,1)} async-done(((bf16[32,1024]{1,0:T(8,128)(2,1)}), bf16[512,1024]{1,0:T(8,128)(2,1)}) %all-gather.10.cloned.1.call-update) | async-done | bytes 1048592 | tf_op jit(solution)/shard_map/all_gather | solution.py:160
  238.1 15.0 %scatter_custom_fusion = bf16[1280,1024]{1,0:T(8,128)(2,1)} fusion(s32[1024]{0:T(1024)S(1)} %bitcast.226, bf16[128,1024]{1,0:T(8,128)(2,1)S(1)} %multiply_convert_fusion, s32[1024]{0:T(1024)S(1)} %broadcast_clamp_fusion.1, bf16[]{:T(256)} %constant.153.clone.1), kind=kCustom, calls=%fused_computation.18 | custom fusion | bytes 2621442 | tf_op jit(solution)/shard_map/scatter | solution.py:176
  253.1 12.9 %all-to-all-start = ((bf16[32,40,1024]{2,1,0:T(8,128)(2,1)}), bf16[32,40,1024]{2,1,0:T(8,128)(2,1)S(1)}, u32[]{:S(2)}, u32[]{:S(2)}) async-start(bf16[32,40,1024]{2,1,0:T(8,128)(2,1)} %bitcast.210), calls=%async_computation | async-start | bytes 5242880 | tf_op jit(solution)/shard_map/all_to_all | solution.py:178
  269.1 6.2 collective-permute-start
  278.8 7.2 %collective-permute-start.2 = (bf16[1,64,1024]{2,1,0:T(8,128)(2,1)S(1)}, bf16[1,64,1024]{2,1,0:T(8,128)(2,1)S(1)}, u32[]{:S(2)}, u32[]{:S(2)}) collective-permute-start(bf16[1,64,1024]{2,1,0:T(8,128)(2,1)S(1)} %collective-permute-done), channel_id=1, source_target_pairs={{0,480},{32,0},{64,32},{96,64},{128,96},{160,128},{192,160},{224,1... | collective-permute-start | bytes 393224 | tf_op jit(solution)/shard_map/ppermute | solution.py:29
  289.0 7.2 %collective-permute-start.4 = (bf16[1,64,1024]{2,1,0:T(8,128)(2,1)S(1)}, bf16[1,64,1024]{2,1,0:T(8,128)(2,1)S(1)}, u32[]{:S(2)}, u32[]{:S(2)}) collective-permute-start(bf16[1,64,1024]{2,1,0:T(8,128)(2,1)S(1)} %collective-permute-done.2), channel_id=1, source_target_pairs={{0,480},{32,0},{64,32},{96,64},{128,96},{160,128},{192,160},{224,1... | collective-permute-start | bytes 393224 | tf_op jit(solution)/shard_map/ppermute | solution.py:29
  299.2 7.2 %collective-permute-start.6 = (bf16[1,64,1024]{2,1,0:T(8,128)(2,1)S(1)}, bf16[1,64,1024]{2,1,0:T(8,128)(2,1)S(1)}, u32[]{:S(2)}, u32[]{:S(2)}) collective-permute-start(bf16[1,64,1024]{2,1,0:T(8,128)(2,1)S(1)} %collective-permute-done.4), channel_id=1, source_target_pairs={{0,480},{32,0},{64,32},{96,64},{128,96},{160,128},{192,160},{224,1... | collective-permute-start | bytes 393224 | tf_op jit(solution)/shard_map/ppermute | solution.py:29
  309.4 7.2 %collective-permute-start.8 = (bf16[1,64,1024]{2,1,0:T(8,128)(2,1)S(1)}, bf16[1,64,1024]{2,1,0:T(8,128)(2,1)}, u32[]{:S(2)}, u32[]{:S(2)}) collective-permute-start(bf16[1,64,1024]{2,1,0:T(8,128)(2,1)S(1)} %collective-permute-done.6), channel_id=1, source_target_pairs={{0,480},{32,0},{64,32},{96,64},{128,96},{160,128},{192,160},{224,1... | collective-permute-start | bytes 393224 | tf_op jit(solution)/shard_map/ppermute | solution.py:29
  319.6 7.4 %collective-permute-start.10 = (bf16[1,64,1024]{2,1,0:T(8,128)(2,1)}, bf16[1,64,1024]{2,1,0:T(8,128)(2,1)}, u32[]{:S(2)}, u32[]{:S(2)}) collective-permute-start(bf16[1,64,1024]{2,1,0:T(8,128)(2,1)} %collective-permute-done.8), channel_id=1, source_target_pairs={{0,480},{32,0},{64,32},{96,64},{128,96},{160,128},{192,160},{224,1... | collective-permute-start | bytes 393224 | tf_op jit(solution)/shard_map/ppermute | solution.py:29
  330.1 7.3 %collective-permute-start.12 = (bf16[1,64,1024]{2,1,0:T(8,128)(2,1)}, bf16[1,64,1024]{2,1,0:T(8,128)(2,1)}, u32[]{:S(2)}, u32[]{:S(2)}) collective-permute-start(bf16[1,64,1024]{2,1,0:T(8,128)(2,1)} %collective-permute-done.10), channel_id=1, source_target_pairs={{0,480},{32,0},{64,32},{96,64},{128,96},{160,128},{192,160},{224,1... | collective-permute-start | bytes 393224 | tf_op jit(solution)/shard_map/ppermute | solution.py:29
  340.5 48.4 %all-to-all-done = bf16[32,40,1024]{2,1,0:T(8,128)(2,1)S(1)} async-done(((bf16[32,40,1024]{2,1,0:T(8,128)(2,1)}), bf16[32,40,1024]{2,1,0:T(8,128)(2,1)S(1)}, u32[]{:S(2)}, u32[]{:S(2)}) %all-to-all-start) | async-done | bytes 2621472 | tf_op jit(solution)/shard_map/all_to_all | solution.py:178
  396.2 4.2 fusion.35
  403.5 4.1 fusion.39
  441.6 27.6 %add_bitcast_fusion = f32[1,1280,1024]{2,1,0:T(8,128)} fusion(f32[1280,1024]{1,0:T(8,128)} %fusion.29, f32[1280,1024]{1,0:T(8,128)} %fusion.31, f32[1280,1024]{1,0:T(8,128)} %fusion.33, f32[1280,1024]{1,0:T(8,128)} %fusion.35, f32[1280,1024]{1,0:T(8,128)} %fusion.37, f32[1280,1024]{1,0:T(8,128)} %fusion.39, f32[1280,1024]{1,0:T(8,128)} %fusion.41, ...), kind=kOutput, calls=%fused_computation.10 | convolution fusion | flops 187432960 | bytes 84344832 | tf_op jit(solution)/shard_map/erd,edf->erf/dot_general | solution.py:186
  469.2 4.4 fusion.7
  473.6 18.2 %copy.137 = bf16[1,1280,1024]{2,0,1:T(2,128)(2,1)} copy(bf16[1,1280,1024]{2,1,0:T(8,128)(2,1)S(1)} %fusion.7) | data formatting | bytes 5242880 | tf_op jit(solution)/shard_map/convert_element_type | solution.py:200
  492.3 15.6 %reduce = bf16[1280,1024]{1,0:T(8,128)(2,1)S(1)} reduce(bf16[1280,1,1024]{2,1,0:T(2,128)(2,1)} %bitcast.207, bf16[]{:T(256)} %broadcast.312), dimensions={1}, to_apply=%bitcast.189.reduce_sub_computation | reduce | bytes 5242882
  515.0 122.2 %all-to-all-done.1 = bf16[32,2,20480]{2,1,0:T(2,128)(2,1)S(1)} async-done(((bf16[32,2,20480]{2,1,0:T(2,128)(2,1)}), bf16[32,2,20480]{2,1,0:T(2,128)(2,1)S(1)}, u32[]{:S(2)}, u32[]{:S(2)}) %all-to-all-start.1) | async-done | bytes 2621472 | tf_op jit(solution)/shard_map/all_to_all | solution.py:201
  637.2 7.2 %reshape.536 = bf16[1280,1,1024]{2,1,0:T(2,128)(2,1)} reshape(bf16[32,2,20480]{2,1,0:T(2,128)(2,1)S(1)} %all-to-all-done.1) | data formatting | bytes 5242880
  647.9 5.4 gather_fusion
  (165 shorter events, 106.5 us)
Async XLA Ops:
  7.2 94.1 %all-gather.6.cloned.1.call-start = ((), (), s32[]{:S(2)}) async-start(), calls=%async_computation.2 | async-start | bytes 2228224 | tf_op jit(solution)/shard_map/all_gather | solution.py:121
  42.3 62.3 %copy-start.22 = (bf16[32,32]{1,0:T(8,128)(2,1)S(1)}, bf16[32,32]{1,0:T(8,128)(2,1)}, u32[]{:S(2)}) copy-start(bf16[32,32]{1,0:T(8,128)(2,1)} %param.18) | copy-start | bytes 6148
  43.1 147.3 %all-gather.8.cloned.1.call-start = ((), (), s32[]{:S(2)}) async-start(), calls=%async_computation.3 | async-start | bytes 4325376 | tf_op jit(solution)/shard_map/all_gather | solution.py:147
  46.0 90.1 %copy-start.21 = (s32[1,128,8]{1,2,0:T(8,128)S(1)}, s32[1,128,8]{1,2,0:T(8,128)}, u32[]{:S(2)}) copy-start(s32[1,128,8]{1,2,0:T(8,128)} %param.14) | copy-start | bytes 12292
  104.5 131.8 %all-gather.10.cloned.1.call-start = ((), (), s32[]{:S(2)}) async-start(), calls=%async_computation.4 | async-start | bytes 1114112 | tf_op jit(solution)/shard_map/all_gather | solution.py:160
  137.0 9.2 %copy-start.20 = (bf16[1,16,512]{2,1,0:T(8,128)(2,1)S(1)}, bf16[1,16,512]{2,1,0:T(8,128)(2,1)}, u32[]{:S(2)}) copy-start(bf16[1,16,512]{2,1,0:T(8,128)(2,1)} %param.13) | copy-start | bytes 49156
  207.8 6.3 copy-start
  223.3 13.0 %copy-start.2 = (bf16[1,128,1024]{2,1,0:T(8,128)(2,1)S(1)}, bf16[1,128,1024]{2,1,0:T(8,128)(2,1)}, u32[]{:S(2)}) copy-start(bf16[1,128,1024]{2,1,0:T(8,128)(2,1)} %param.11) | copy-start | bytes 786436
  223.3 14.7 %copy-start.23 = (f32[1024]{0:T(1024)S(1)}, f32[1024]{0:T(1024)}, u32[]{:S(2)}) copy-start(f32[1024]{0:T(1024)} %param.19) | copy-start | bytes 12292
  253.1 13.0 %copy-start.3 = (bf16[1,64,1024]{2,1,0:T(8,128)(2,1)S(1)}, bf16[1,64,1024]{2,1,0:T(8,128)(2,1)}, u32[]{:S(2)}) copy-start(bf16[1,64,1024]{2,1,0:T(8,128)(2,1)} %param.20) | copy-start | bytes 393220
  253.1 135.7 %all-to-all-start = ((bf16[32,40,1024]{2,1,0:T(8,128)(2,1)}), bf16[32,40,1024]{2,1,0:T(8,128)(2,1)S(1)}, u32[]{:S(2)}, u32[]{:S(2)}) async-start(bf16[32,40,1024]{2,1,0:T(8,128)(2,1)} %bitcast.210), calls=%async_computation | async-start | bytes 5242880 | tf_op jit(solution)/shard_map/all_to_all | solution.py:178
  266.1 203.1 %all-gather.12.cloned.1.call-start = ((), (), s32[]{:S(2)}) async-start(), calls=%async_computation.5 | async-start | bytes 1114112 | tf_op jit(solution)/shard_map/all_gather | solution.py:198
  266.1 10.8 %collective-permute-start.1 = (bf16[1,64,1024]{2,1,0:T(8,128)(2,1)S(1)}, bf16[1,64,1024]{2,1,0:T(8,128)(2,1)S(1)}, u32[]{:S(2)}, u32[]{:S(2)}) collective-permute-start(bf16[1,64,1024]{2,1,0:T(8,128)(2,1)S(1)} %copy-done.3), channel_id=1, source_target_pairs={{0,32},{32,64},{64,96},{96,128},{128,160},{160,192},{192,224},{224... | collective-permute-start | bytes 393224 | tf_op jit(solution)/shard_map/ppermute | solution.py:27
  269.1 9.7 %collective-permute-start = (bf16[1,64,1024]{2,1,0:T(8,128)(2,1)S(1)}, bf16[1,64,1024]{2,1,0:T(8,128)(2,1)S(1)}, u32[]{:S(2)}, u32[]{:S(2)}) collective-permute-start(bf16[1,64,1024]{2,1,0:T(8,128)(2,1)S(1)} %copy-done.3), channel_id=1, source_target_pairs={{0,480},{32,0},{64,32},{96,64},{128,96},{160,128},{192,160},{224,1... | collective-permute-start | bytes 393224 | tf_op jit(solution)/shard_map/ppermute | solution.py:29
  276.9 10.2 %collective-permute-start.3 = (bf16[1,64,1024]{2,1,0:T(8,128)(2,1)S(1)}, bf16[1,64,1024]{2,1,0:T(8,128)(2,1)S(1)}, u32[]{:S(2)}, u32[]{:S(2)}) collective-permute-start(bf16[1,64,1024]{2,1,0:T(8,128)(2,1)S(1)} %collective-permute-done.1), channel_id=1, source_target_pairs={{0,32},{32,64},{64,96},{96,128},{128,160},{160,192},{192,224},{224... | collective-permute-start | bytes 393224 | tf_op jit(solution)/shard_map/ppermute | solution.py:27
  278.8 58.6 %copy-start.4 = (bf16[1,64,1024]{2,1,0:T(8,128)(2,1)}, bf16[1,64,1024]{2,1,0:T(8,128)(2,1)S(1)}, u32[]{:S(2)}) copy-start(bf16[1,64,1024]{2,1,0:T(8,128)(2,1)S(1)} %collective-permute-done) | copy-start | bytes 393220
  278.8 10.2 %collective-permute-start.2 = (bf16[1,64,1024]{2,1,0:T(8,128)(2,1)S(1)}, bf16[1,64,1024]{2,1,0:T(8,128)(2,1)S(1)}, u32[]{:S(2)}, u32[]{:S(2)}) collective-permute-start(bf16[1,64,1024]{2,1,0:T(8,128)(2,1)S(1)} %collective-permute-done), channel_id=1, source_target_pairs={{0,480},{32,0},{64,32},{96,64},{128,96},{160,128},{192,160},{224,1... | collective-permute-start | bytes 393224 | tf_op jit(solution)/shard_map/ppermute | solution.py:29
  287.1 10.2 %collective-permute-start.5 = (bf16[1,64,1024]{2,1,0:T(8,128)(2,1)S(1)}, bf16[1,64,1024]{2,1,0:T(8,128)(2,1)S(1)}, u32[]{:S(2)}, u32[]{:S(2)}) collective-permute-start(bf16[1,64,1024]{2,1,0:T(8,128)(2,1)S(1)} %collective-permute-done.3), channel_id=1, source_target_pairs={{0,32},{32,64},{64,96},{96,128},{128,160},{160,192},{192,224},{224... | collective-permute-start | bytes 393224 | tf_op jit(solution)/shard_map/ppermute | solution.py:27
  289.0 8.2 %copy-start.8 = (bf16[1,64,1024]{2,1,0:T(8,128)(2,1)}, bf16[1,64,1024]{2,1,0:T(8,128)(2,1)S(1)}, u32[]{:S(2)}) copy-start(bf16[1,64,1024]{2,1,0:T(8,128)(2,1)S(1)} %collective-permute-done.2) | copy-start | bytes 393220
  289.0 10.1 %collective-permute-start.4 = (bf16[1,64,1024]{2,1,0:T(8,128)(2,1)S(1)}, bf16[1,64,1024]{2,1,0:T(8,128)(2,1)S(1)}, u32[]{:S(2)}, u32[]{:S(2)}) collective-permute-start(bf16[1,64,1024]{2,1,0:T(8,128)(2,1)S(1)} %collective-permute-done.2), channel_id=1, source_target_pairs={{0,480},{32,0},{64,32},{96,64},{128,96},{160,128},{192,160},{224,1... | collective-permute-start | bytes 393224 | tf_op jit(solution)/shard_map/ppermute | solution.py:29
  297.3 10.2 %collective-permute-start.7 = (bf16[1,64,1024]{2,1,0:T(8,128)(2,1)S(1)}, bf16[1,64,1024]{2,1,0:T(8,128)(2,1)S(1)}, u32[]{:S(2)}, u32[]{:S(2)}) collective-permute-start(bf16[1,64,1024]{2,1,0:T(8,128)(2,1)S(1)} %collective-permute-done.5), channel_id=1, source_target_pairs={{0,32},{32,64},{64,96},{96,128},{128,160},{160,192},{192,224},{224... | collective-permute-start | bytes 393224 | tf_op jit(solution)/shard_map/ppermute | solution.py:27
  299.2 8.2 %copy-start.12 = (bf16[1,64,1024]{2,1,0:T(8,128)(2,1)}, bf16[1,64,1024]{2,1,0:T(8,128)(2,1)S(1)}, u32[]{:S(2)}) copy-start(bf16[1,64,1024]{2,1,0:T(8,128)(2,1)S(1)} %collective-permute-done.4) | copy-start | bytes 393220
  299.2 10.1 %collective-permute-start.6 = (bf16[1,64,1024]{2,1,0:T(8,128)(2,1)S(1)}, bf16[1,64,1024]{2,1,0:T(8,128)(2,1)S(1)}, u32[]{:S(2)}, u32[]{:S(2)}) collective-permute-start(bf16[1,64,1024]{2,1,0:T(8,128)(2,1)S(1)} %collective-permute-done.4), channel_id=1, source_target_pairs={{0,480},{32,0},{64,32},{96,64},{128,96},{160,128},{192,160},{224,1... | collective-permute-start | bytes 393224 | tf_op jit(solution)/shard_map/ppermute | solution.py:29
  307.4 10.2 %collective-permute-start.9 = (bf16[1,64,1024]{2,1,0:T(8,128)(2,1)S(1)}, bf16[1,64,1024]{2,1,0:T(8,128)(2,1)S(1)}, u32[]{:S(2)}, u32[]{:S(2)}) collective-permute-start(bf16[1,64,1024]{2,1,0:T(8,128)(2,1)S(1)} %collective-permute-done.7), channel_id=1, source_target_pairs={{0,32},{32,64},{64,96},{96,128},{128,160},{160,192},{192,224},{224... | collective-permute-start | bytes 393224 | tf_op jit(solution)/shard_map/ppermute | solution.py:27
  309.4 8.2 %copy-start.16 = (bf16[1,64,1024]{2,1,0:T(8,128)(2,1)}, bf16[1,64,1024]{2,1,0:T(8,128)(2,1)S(1)}, u32[]{:S(2)}) copy-start(bf16[1,64,1024]{2,1,0:T(8,128)(2,1)S(1)} %collective-permute-done.6) | copy-start | bytes 393220
  309.4 10.1 %collective-permute-start.8 = (bf16[1,64,1024]{2,1,0:T(8,128)(2,1)S(1)}, bf16[1,64,1024]{2,1,0:T(8,128)(2,1)}, u32[]{:S(2)}, u32[]{:S(2)}) collective-permute-start(bf16[1,64,1024]{2,1,0:T(8,128)(2,1)S(1)} %collective-permute-done.6), channel_id=1, source_target_pairs={{0,480},{32,0},{64,32},{96,64},{128,96},{160,128},{192,160},{224,1... | collective-permute-start | bytes 393224 | tf_op jit(solution)/shard_map/ppermute | solution.py:29
  317.6 10.3 %collective-permute-start.11 = (bf16[1,64,1024]{2,1,0:T(8,128)(2,1)S(1)}, bf16[1,64,1024]{2,1,0:T(8,128)(2,1)}, u32[]{:S(2)}, u32[]{:S(2)}) collective-permute-start(bf16[1,64,1024]{2,1,0:T(8,128)(2,1)S(1)} %collective-permute-done.9), channel_id=1, source_target_pairs={{0,32},{32,64},{64,96},{96,128},{128,160},{160,192},{192,224},{224... | collective-permute-start | bytes 393224 | tf_op jit(solution)/shard_map/ppermute | solution.py:27
  319.6 10.6 %collective-permute-start.10 = (bf16[1,64,1024]{2,1,0:T(8,128)(2,1)}, bf16[1,64,1024]{2,1,0:T(8,128)(2,1)}, u32[]{:S(2)}, u32[]{:S(2)}) collective-permute-start(bf16[1,64,1024]{2,1,0:T(8,128)(2,1)} %collective-permute-done.8), channel_id=1, source_target_pairs={{0,480},{32,0},{64,32},{96,64},{128,96},{160,128},{192,160},{224,1... | collective-permute-start | bytes 393224 | tf_op jit(solution)/shard_map/ppermute | solution.py:29
  327.9 10.5 %collective-permute-start.13 = (bf16[1,64,1024]{2,1,0:T(8,128)(2,1)}, bf16[1,64,1024]{2,1,0:T(8,128)(2,1)}, u32[]{:S(2)}, u32[]{:S(2)}) collective-permute-start(bf16[1,64,1024]{2,1,0:T(8,128)(2,1)} %collective-permute-done.11), channel_id=1, source_target_pairs={{0,32},{32,64},{64,96},{96,128},{128,160},{160,192},{192,224},{224... | collective-permute-start | bytes 393224 | tf_op jit(solution)/shard_map/ppermute | solution.py:27
  330.1 107.4 %collective-permute-start.12 = (bf16[1,64,1024]{2,1,0:T(8,128)(2,1)}, bf16[1,64,1024]{2,1,0:T(8,128)(2,1)}, u32[]{:S(2)}, u32[]{:S(2)}) collective-permute-start(bf16[1,64,1024]{2,1,0:T(8,128)(2,1)} %collective-permute-done.10), channel_id=1, source_target_pairs={{0,480},{32,0},{64,32},{96,64},{128,96},{160,128},{192,160},{224,1... | collective-permute-start | bytes 393224 | tf_op jit(solution)/shard_map/ppermute | solution.py:29
  338.4 103.2 %collective-permute-start.14 = (bf16[1,64,1024]{2,1,0:T(8,128)(2,1)}, bf16[1,64,1024]{2,1,0:T(8,128)(2,1)S(1)}, u32[]{:S(2)}, u32[]{:S(2)}) collective-permute-start(bf16[1,64,1024]{2,1,0:T(8,128)(2,1)} %collective-permute-done.13), channel_id=1, source_target_pairs={{0,32},{32,64},{64,96},{96,128},{128,160},{160,192},{192,224},{224... | collective-permute-start | bytes 393224 | tf_op jit(solution)/shard_map/ppermute | solution.py:27
  510.9 126.3 %all-to-all-start.1 = ((bf16[32,2,20480]{2,1,0:T(2,128)(2,1)}), bf16[32,2,20480]{2,1,0:T(2,128)(2,1)S(1)}, u32[]{:S(2)}, u32[]{:S(2)}) async-start(bf16[32,2,20480]{2,1,0:T(2,128)(2,1)} %reshape.535), calls=%async_computation.1 | async-start | bytes 5242880 | tf_op jit(solution)/shard_map/all_to_all | solution.py:201
  (14 other events, 45.6 us)
Sparse Core Ops, SparseCore 0:
  43.2 58.0 all-gather.5
  104.6 74.1 all-gather.7
  181.8 54.5 all-gather.9
  330.0 58.6 all-gather.11
